TPU v7x, 128 devices: a whole 4x4x4 slice. The times are simulated.
128 devices in a mesh: req: 16 (over z, x_lo, core), blk: 8 (over y, x_hi).
Axes of the slice: x: 4 (x_hi: 2, x_lo: 2; x = x_hi * 2 + x_lo), y: 4, z: 4, core: 2. Of those that a mesh axis runs over, the one named last changes fastest.
Arguments:
- prefill_rows: bfloat16 [8, 16, 256, 1536], P('blk', 'req'), may hold values from -3 to 3
- decode_rows: bfloat16 [8, 16, 16, 1536], P('blk', 'req'), may hold values from -3 to 3
- cache_pool: bfloat16 [8, 16, 408, 16, 512], P('blk', 'req'), may hold values from -300 to 300
- page_table: int32 [8, 16, 17, 24], P('blk', 'req'), may hold values from 0 to 407, as said below
- lengths: int32 [8, 16, 17], P('blk', 'req'), may hold values from 1 to 383, as said below
- destination: int32 [8, 16, 16], P('blk', 'req'), may hold values from 0 to 15, as said below
- attn_gain: bfloat16 [1536], replicated, may hold values from 0.5 to 1.5
- inproj_weight: bfloat16 [1536, 2048], replicated, may hold values from -0.15625 to 0.15625
- inproj_bias: bfloat16 [2048], replicated, may hold values from -3 to 3
- outproj_weight: bfloat16 [1536, 1536], replicated, may hold values from -0.15625 to 0.15625
- mlp_gain: bfloat16 [1536], replicated, may hold values from 0.5 to 1.5
- gate_up: bfloat16 [1536, 2, 8960], P('req', None, 'blk'), may hold values from -0.15625 to 0.15625
- down_weight: bfloat16 [8960, 1536], P('blk', 'req'), may hold values from -0.0625 to 0.0625
Outputs:
- prefill_out: bfloat16 [8, 16, 256, 1536], P('blk', 'req')
- decode_out: bfloat16 [8, 16, 16, 1536], P('blk', 'req')
- new_cache: bfloat16 [8, 16, 16, 384, 512], P('blk', 'req')
Inputs may be any that keep to these rules, and one draw needn't show every extreme that they name: Each device sends exactly 0 or 2 of its decode requests to each index of req and receives exactly 16; destination minus source index, modulo the size of req, depends only on the blk index and the slot. `lengths`: slot 16 is the prefill request's context. Every device holds a decode request of length 383. `page_table`: on each device a permutation of its 408 pages.
All inputs are finite; a program needn't handle non-finite values.
Results may differ from a plain program's by a relative error of at most 0.024.
Values may be sent and summed in bfloat16 or wider, within the bound.
A program may use at most 192 MiB of HBM per device.

v0:
```python
import math

import jax
import jax.numpy as jnp
from jax import lax
from jax.sharding import PartitionSpec as P

QUERY_HEADS = 12
KEY_VALUE_HEADS = 2
HEAD_SIZE = 128
CAP = 2


rms_eps = 1e-06
rope_base = 1000000.0


def rms_scale(rows, gain_row):
    rows_wide = rows.astype(jnp.float32)
    inverse = lax.rsqrt(jnp.mean(rows_wide * rows_wide, axis=-1, keepdims=True) + rms_eps)
    return (rows_wide * inverse * gain_row.astype(jnp.float32)).astype(jnp.bfloat16)


def apply_rotary(vectors, token_positions):
    head_dim = vectors.shape[-1]
    half_dim = head_dim // 2
    frequency = rope_base ** (-2.0 * jnp.arange(half_dim, dtype=jnp.float32) / head_dim)
    angles = token_positions.astype(jnp.float32)[:, None] * frequency[None, :]
    cosine = jnp.concatenate([jnp.cos(angles), jnp.cos(angles)], axis=-1)[:, None, :]
    sine_table = jnp.concatenate([jnp.sin(angles), jnp.sin(angles)], axis=-1)[:, None, :]
    turned = jnp.concatenate([-vectors[..., half_dim:], vectors[..., :half_dim]], axis=-1)
    return vectors * cosine + turned * sine_table


def project(normed, weight, bias_row, token_positions):
    mixed_batch = jnp.dot(normed, weight, preferred_element_type=jnp.float32) + bias_row.astype(
        jnp.float32
    )
    query_head_width = QUERY_HEADS * HEAD_SIZE
    key_head_width = KEY_VALUE_HEADS * HEAD_SIZE
    query_rows = apply_rotary(
        mixed_batch[:, :query_head_width].reshape(-1, QUERY_HEADS, HEAD_SIZE), token_positions
    )
    key_row_block = apply_rotary(
        mixed_batch[:, query_head_width : query_head_width + key_head_width].reshape(
            -1, KEY_VALUE_HEADS, HEAD_SIZE
        ),
        token_positions,
    )
    value_rows = mixed_batch[:, query_head_width + key_head_width :]
    key_value_pair = jnp.concatenate(
        [key_row_block.reshape(-1, key_head_width), value_rows], axis=-1
    )
    return (
        query_rows.reshape(-1, query_head_width).astype(jnp.bfloat16),
        key_value_pair.astype(jnp.bfloat16),
    )


def attend(query_rows, key_value_pair, allowed):
    batch_count = query_rows.shape[0]
    total_rows = query_rows.shape[1]
    group_width = QUERY_HEADS // KEY_VALUE_HEADS
    key_head_width = KEY_VALUE_HEADS * HEAD_SIZE
    grouped_heads = query_rows.reshape(
        batch_count, total_rows, KEY_VALUE_HEADS, group_width, HEAD_SIZE
    )
    key_row_block = key_value_pair[:, :, :key_head_width].reshape(
        batch_count, -1, KEY_VALUE_HEADS, HEAD_SIZE
    )
    value_rows = key_value_pair[:, :, key_head_width:].reshape(
        batch_count, -1, KEY_VALUE_HEADS, HEAD_SIZE
    )
    scores = jnp.einsum(
        "bqhgd,bkhd->bhgqk", grouped_heads, key_row_block, preferred_element_type=jnp.float32
    ) / math.sqrt(HEAD_SIZE)
    scores = jnp.where(allowed[:, None, None, :, :], scores, -jnp.inf)
    row_max = jnp.max(scores, axis=-1, keepdims=True)
    weights = jnp.exp(scores - row_max)
    weights = (weights / jnp.sum(weights, axis=-1, keepdims=True)).astype(jnp.bfloat16)
    result = jnp.einsum(
        "bhgqk,bkhd->bqhgd", weights, value_rows, preferred_element_type=jnp.float32
    )
    return result.reshape(batch_count, total_rows, QUERY_HEADS * HEAD_SIZE).astype(jnp.bfloat16)


def extend(cache_rows, key_value_pair, lengths_now):
    token_positions = jnp.arange(cache_rows.shape[1], dtype=jnp.int32)[None, :, None]
    limit = lengths_now[:, None, None]
    return jnp.where(
        token_positions < limit,
        cache_rows,
        jnp.where(token_positions == limit, key_value_pair[:, None, :], jnp.zeros_like(cache_rows)),
    )


def shards(
    prefill_rows,
    decode_rows,
    cache_pool,
    page_table,
    lengths,
    destination,
    attn_gain,
    inproj_weight,
    inproj_bias,
    outproj_weight,
    mlp_gain,
    gate_up,
    down_weight,
):
    n_req = lax.axis_size("req")
    own_index = lax.axis_index("req")
    slot_total = destination.shape[2]
    pool_rows = cache_pool[0, 0]
    table_rows = page_table[0, 0]
    width_per_row = pool_rows.shape[-1]
    gathered = pool_rows[table_rows].reshape(slot_total + 1, -1, width_per_row)
    cache_length = gathered.shape[1]
    decode_caches = gathered[:slot_total]
    context = gathered[slot_total]
    context_length = lengths[0, 0, slot_total]
    slot_ids = jnp.arange(slot_total, dtype=jnp.int32)
    all_dest, all_len = (
        lax.all_gather(destination, "req", axis=1, tiled=True),
        lax.all_gather(lengths, "req", axis=1, tiled=True),
    )
    all_dest = all_dest[0]
    all_len = all_len[0]
    prefill_x = prefill_rows[0, 0]
    prefill_count = prefill_x.shape[0]
    block_ids = jnp.arange(prefill_count, dtype=jnp.int32)
    cache_ids = jnp.arange(cache_length, dtype=jnp.int32)
    prefill_q, prefill_kv = project(
        rms_scale(prefill_x, attn_gain), inproj_weight, inproj_bias, context_length + block_ids
    )
    key_block = jnp.concatenate([context, prefill_kv], axis=0)
    allowed = jnp.concatenate(
        [
            jnp.broadcast_to(cache_ids[None, :] < context_length, (prefill_count, cache_length)),
            block_ids[None, :] <= block_ids[:, None],
        ],
        axis=1,
    )
    prefill_att = attend(prefill_q[None], key_block[None], allowed[None])[0]
    send_dest = destination[0, 0]
    decode_x = decode_rows[0, 0]
    earlier = (send_dest[None, :] == send_dest[:, None]) & (slot_ids[None, :] < slot_ids[:, None])
    within = jnp.sum(earlier.astype(jnp.int32), axis=1)
    target = send_dest * CAP + within
    flat_slots = jnp.arange(n_req * CAP, dtype=jnp.int32)
    matches = target[None, :] == flat_slots[:, None]
    picked = jnp.sum(jnp.where(matches, slot_ids[None, :], 0), axis=1)
    filled = jnp.any(matches, axis=1)
    send_cache = jnp.where(
        filled[:, None, None], decode_caches[picked], jnp.zeros((), jnp.bfloat16)
    ).reshape(n_req, CAP, cache_length, width_per_row)
    send_x = jnp.where(filled[:, None], decode_x[picked], jnp.zeros((), jnp.bfloat16)).reshape(
        n_req, CAP, -1
    )
    recv_cache, recv_x = (
        lax.all_to_all(send_cache, "req", split_axis=0, concat_axis=0, tiled=True),
        lax.all_to_all(send_x, "req", split_axis=0, concat_axis=0, tiled=True),
    )
    arriving = all_dest == own_index
    arrival_rank = jnp.cumsum(arriving.astype(jnp.int32), axis=1) - 1
    cap_ids = jnp.arange(CAP, dtype=jnp.int32)
    placed = arriving[:, None, :] & (arrival_rank[:, None, :] == cap_ids[None, :, None])
    slot_lengths = jnp.sum(jnp.where(placed, all_len[:, None, :slot_total], 0), axis=2).reshape(-1)
    valid = jnp.any(placed, axis=2).reshape(-1)
    position = jnp.cumsum(valid.astype(jnp.int32)) - 1
    chosen = valid[None, :] & (position[None, :] == slot_ids[:, None])
    arrival_order = jnp.sum(jnp.where(chosen, flat_slots[None, :], 0), axis=1)
    got_cache = recv_cache.reshape(n_req * CAP, cache_length, width_per_row)[arrival_order]
    got_x = recv_x.reshape(n_req * CAP, -1)[arrival_order]
    got_length = slot_lengths[arrival_order]
    decode_q, decode_kv = project(
        rms_scale(got_x, attn_gain), inproj_weight, inproj_bias, got_length
    )
    cache_after = extend(got_cache, decode_kv, got_length)
    decode_allowed = (cache_ids[None, :] <= got_length[:, None])[:, None, :]
    decode_att = attend(decode_q[:, None, :], cache_after, decode_allowed)[:, 0]
    inputs_all = jnp.concatenate([prefill_x, got_x], axis=0)
    attended = jnp.concatenate([prefill_att, decode_att], axis=0)
    residual = inputs_all.astype(jnp.float32) + jnp.dot(
        attended, outproj_weight, preferred_element_type=jnp.float32
    )
    mlp_in = rms_scale(residual, mlp_gain)
    full_gate_up, full_down = (
        lax.all_gather(gate_up, "req", axis=0, tiled=True),
        lax.all_gather(down_weight, "req", axis=1, tiled=True),
    )
    gate_and_up = jnp.einsum(
        "nd,dkf->nkf",
        lax.all_gather(mlp_in, "blk", axis=0, tiled=True),
        full_gate_up,
        preferred_element_type=jnp.float32,
    )
    hidden = (jax.nn.silu(gate_and_up[:, 0, :]) * gate_and_up[:, 1, :]).astype(jnp.bfloat16)
    mlp_rows = lax.psum_scatter(
        jnp.dot(hidden, full_down, preferred_element_type=jnp.float32).astype(jnp.bfloat16),
        "blk",
        scatter_dimension=0,
        tiled=True,
    ).astype(jnp.float32)
    layer_rows = (residual + mlp_rows).astype(jnp.bfloat16)
    return (
        layer_rows[:prefill_count][None, None],
        layer_rows[prefill_count:][None, None],
        cache_after[None, None],
    )


def solution(mesh):
    return jax.shard_map(
        shards,
        mesh=mesh,
        in_specs=(
            P("blk", "req", None, None),
            P("blk", "req", None, None),
            P("blk", "req", None, None, None),
            P("blk", "req", None, None),
            P("blk", "req", None),
            P("blk", "req", None),
            P(),
            P(),
            P(),
            P(),
            P(),
            P("req", None, "blk"),
            P("blk", "req"),
        ),
        out_specs=(
            P("blk", "req", None, None),
            P("blk", "req", None, None),
            P("blk", "req", None, None, None),
        ),
        check_vma=False,
    )
```

profile of v0, /device:TPU:0, one launch (start us, length us, event | category | flops | bytes accessed | tf_op | source)
XLA Modules:
  0.0 633.0 jit_solution(8408661679240010259)
XLA Ops:
  7.2 0.9 convert_reduce_fusion
  8.1 0.7 multiply_add_fusion
  9.0 0.6 gather_fusion
  9.7 0.8 broadcast_select_fusion.1
  10.6 6.4 %all-to-all-start = ((bf16[16,2,1536]{2,1,0:T(2,128)(2,1)}), bf16[16,2,1536]{2,1,0:T(2,128)(2,1)S(1)}, u32[]{:S(2)}, u32[]{:S(2)}) async-start(bf16[16,2,1536]{2,1,0:T(2,128)(2,1)} %broadcast_select_fusion.1), calls=%async_computation | async-start | bytes 196608 | tf_op jit(solution)/shard_map/all_to_all | solution.py:163
  17.0 0.7 fusion.39
  17.8 22.5 %gather_fusion.2 = bf16[408,16,512]{2,1,0:T(8,128)(2,1)} fusion(bf16[408,16,512]{2,1,0:T(8,128)(2,1)} %bitcast.159, s32[1024]{0:T(1024)S(1)} %pad_clamp_fusion), kind=kCustom, calls=%fused_computation.2 | custom fusion | bytes 13370976 | tf_op jit(solution)/shard_map/gather | solution.py:118
  40.4 6.2 slice.136
  46.6 9.4 %gather_fusion.4 = bf16[32,384,512]{2,1,0:T(8,128)(2,1)} fusion(bf16[16,384,512]{2,1,0:T(8,128)(2,1)} %bitcast.155, s32[1024]{0:T(1024)S(1)} %pad_clamp_fusion.2), kind=kCustom, calls=%fused_computation.4 | custom fusion | bytes 25165952 | tf_op jit(solution)/shard_map/gather | solution.py:156
  56.0 10.7 %broadcast_select_fusion = bf16[16,2,384,512]{3,2,1,0:T(8,128)(2,1)} fusion(bf16[16,2,384,512]{3,2,1,0:T(8,128)(2,1)} %bitcast.156, pred[16,2]{1,0:T(8,128)(4,1)S(1)} %broadcast_in_dim.124), kind=kLoop, calls=%fused_computation.6 | loop fusion | flops 6291456 | bytes 25165856 | tf_op jit(solution)/shard_map/jit(_where)/select_n | solution.py:155
  66.7 5.9 all-to-all-start.1
  72.7 0.8 copy.122
  73.6 0.2 fusion.9
  73.9 4.7 convolution_add_fusion.1
  78.7 1.3 slice.132
  79.9 200.0 %all_gather.15 = s32[1,16,16]{2,0,1:T(1,128)S(1)} all-gather(s32[1,1,16]{2,0,1:T(1,128)S(1)} %bitcast.178), channel_id=1, replica_groups=mesh['req'=16,'blk'=8] {'req'}, dimensions={1}, use_global_device_ids=true | all-gather | bytes 1088 | tf_op jit(solution)/shard_map/all_gather | solution.py:125
  280.3 0.7 copy.101
  281.0 0.6 slice.86
  281.6 0.6 add_convert_fusion.2
  282.2 0.3 multiply_cosine_fusion
  282.6 0.8 copy.105
  283.6 0.3 slice_negate_fusion.1
  283.9 1.3 maximum_multiply_fusion.1
  285.4 0.8 fusion.52
  286.2 0.9 copy.107
  287.1 3.0 copy.109
  290.1 1.5 slice_negate_fusion
  291.6 1.3 maximum_multiply_fusion
  292.9 3.0 copy.110
  295.9 1.3 mul.223
  297.2 3.0 copy.108
  300.2 2.2 add_convert_fusion.1
  302.4 0.3 copy.111
  302.7 1.2 copy.106
  304.2 18.5 %all_gather.16 = s32[1,16,17]{2,0,1:T(1,128)S(1)} all-gather(s32[1,1,17]{2,0,1:T(1,128)S(1)} %bitcast.179), channel_id=1, replica_groups=mesh['req'=16,'blk'=8] {'req'}, dimensions={1}, use_global_device_ids=true | all-gather | bytes 1156 | tf_op jit(solution)/shard_map/all_gather | solution.py:126
  323.2 0.7 gather_fusion.3
  323.9 0.6 iota_compare_fusion.8
  325.0 2.3 fusion.5
  327.3 1.6 fusion.2
  329.0 3.2 fusion.12
  332.3 0.6 gather_fusion.1
  333.0 3.8 convolution_add_fusion.2
  337.5 8.2 %gather_fusion.5 = bf16[16,384,512]{2,1,0:T(8,128)(2,1)} fusion(bf16[32,384,512]{2,1,0:T(8,128)(2,1)} %bitcast.34, s32[1024]{0:T(1024)S(1)} %pad_clamp_fusion.1), kind=kCustom, calls=%fused_computation.5 | custom fusion | bytes 12582976 | tf_op jit(solution)/shard_map/gather | solution.py:174
  345.7 6.1 select_select_fusion
  351.8 3.4 fusion.51
  355.3 3.4 copy.118
  358.7 4.7 copy.117
  363.4 0.8 fusion.53
  364.2 0.2 fusion.25
  364.4 3.1 fusion.21
  367.5 0.3 copy.131
  367.8 4.4 multiply_reduce_fusion
  372.2 1.2 multiply_convert_fusion
  373.4 0.7 all-gather.8.cloned.1.call-update
  374.1 0.2 reduce-scatter.2.cloned.1.call-start
  374.4 89.8 %all-gather.4.cloned.1.call-done = bf16[2176,1536]{1,0:T(8,128)(2,1)} async-done(((bf16[272,1536]{1,0:T(8,128)(2,1)}), bf16[2176,1536]{1,0:T(8,128)(2,1)}) %all-gather.4.cloned.1.call-update) | async-done | bytes 6684688 | tf_op jit(solution)/shard_map/all_gather | solution.py:195
  464.2 23.1 %fusion.3 = f32[2176,2,1120]{0,2,1:T(8,128)} fusion(bf16[1536,2,1120]{2,0,1:T(8,128)(2,1)} %all-gather.6.cloned.1.call-done, bf16[2176,1536]{1,0:T(8,128)(2,1)} %all-gather.4.cloned.1.call-done), kind=kOutput, calls=%fused_computation.16 | convolution fusion | flops 14973665280 | bytes 33062912 | tf_op jit(solution)/shard_map/nd,dkf->nkf/dot_general | solution.py:193
  487.3 13.2 %all-gather.8.cloned.1.call-done = bf16[1120,1536]{0,1:T(8,128)(2,1)} async-done(((bf16[1120,96]{0,1:T(8,128)(2,1)}), bf16[1120,1536]{0,1:T(8,128)(2,1)}) %all-gather.8.cloned.1.call-update) | async-done | bytes 3440656 | tf_op jit(solution)/shard_map/all_gather | solution.py:191
  500.5 20.9 %convolution_convert_fusion = bf16[2176,1536]{1,0:T(8,128)(2,1)} fusion(bf16[1120,1536]{0,1:T(8,128)(2,1)} %all-gather.8.cloned.1.call-done, f32[2176,2,1120]{0,2,1:T(8,128)} %fusion.3), kind=kOutput, calls=%fused_computation.7 | convolution fusion | flops 7504797696 | bytes 29622272 | tf_op jit(solution)/shard_map/dot_general | solution.py:201
  521.4 7.6 %bitcast_select_fusion.1 = bf16[1,1,16,384,512]{4,3,2,1,0:T(8,128)(2,1)} fusion(bf16[16,384,512]{2,1,0:T(8,128)(2,1)} %gather_fusion.5, pred[16,384]{1,0:T(8,128)(4,1)S(1)} %get-tuple-element.25, pred[16,384]{1,0:T(8,128)(4,1)S(1)} %get-tuple-element.26, bf16[16,512]{1,0:T(8,128)(2,1)S(1)} %pad_maximum_fusion.2), kind=kLoop, calls=%fused_computation.18 | loop fusion | flops 6291456 | bytes 12611584 | tf_op jit(solution)/shard_map/jit(_where)/select_n | solution.py:90
  529.0 94.1 %reduce-scatter.2.cloned.1.call-done = bf16[272,1536]{1,0:T(8,128)(2,1)} async-done(((bf16[2176,1536]{1,0:T(8,128)(2,1)}), bf16[272,1536]{1,0:T(8,128)(2,1)}) %reduce-scatter.2.cloned.1.call-update) | async-done | bytes 835600 | tf_op jit(solution)/shard_map/reduce_scatter | solution.py:200
  623.2 1.3 add_convert_fusion
  624.5 0.9 slice_bitcast_fusion.2
  625.5 0.6 slice_bitcast_fusion.3
  (112 shorter events, 3.6 us)
Async XLA Ops:
  7.2 1.8 copy-start
  10.6 56.1 %all-to-all-start = ((bf16[16,2,1536]{2,1,0:T(2,128)(2,1)}), bf16[16,2,1536]{2,1,0:T(2,128)(2,1)S(1)}, u32[]{:S(2)}, u32[]{:S(2)}) async-start(bf16[16,2,1536]{2,1,0:T(2,128)(2,1)} %broadcast_select_fusion.1), calls=%async_computation | async-start | bytes 196608 | tf_op jit(solution)/shard_map/all_to_all | solution.py:163
  66.7 6.0 copy-start.3
  66.7 6.9 %copy-start.11 = (bf16[1536]{0:T(1024)(128)(2,1)S(1)}, bf16[1536]{0:T(1024)(128)(2,1)}, u32[]{:S(2)}) copy-start(bf16[1536]{0:T(1024)(128)(2,1)} %param.19) | copy-start | bytes 9220
  66.7 6.9 %copy-start.12 = (bf16[2048]{0:T(1024)(128)(2,1)S(1)}, bf16[2048]{0:T(1024)(128)(2,1)}, u32[]{:S(2)}) copy-start(bf16[2048]{0:T(1024)(128)(2,1)} %param.21) | copy-start | bytes 12292
  66.7 6.9 %copy-start.2 = (bf16[1,1,256,1536]{3,2,1,0:T(8,128)(2,1)S(1)}, bf16[1,1,256,1536]{3,2,1,0:T(8,128)(2,1)}, u32[]{:S(2)}) copy-start(bf16[1,1,256,1536]{3,2,1,0:T(8,128)(2,1)} %param.13) | copy-start | bytes 2359300
  66.7 270.8 %all-to-all-start.1 = ((bf16[16,2,384,512]{3,2,1,0:T(8,128)(2,1)}), bf16[16,2,384,512]{3,2,1,0:T(8,128)(2,1)}, u32[]{:S(2)}, u32[]{:S(2)}) async-start(bf16[16,2,384,512]{3,2,1,0:T(8,128)(2,1)} %broadcast_select_fusion), calls=%async_computation.1 | async-start | bytes 25165824 | tf_op jit(solution)/shard_map/all_to_all | solution.py:162
  72.6 301.7 %all-gather.6.cloned.1.call-start = ((), (), s32[]{:S(2)}) async-start(), calls=%async_computation.4 | async-start | bytes 7520256 | tf_op jit(solution)/shard_map/all_gather | solution.py:190
  73.5 390.7 %all-gather.4.cloned.1.call-start = ((), (), s32[]{:S(2)}) async-start(), calls=%async_computation.3 | async-start | bytes 7520256 | tf_op jit(solution)/shard_map/all_gather | solution.py:195
  73.6 5.0 copy-start.4
  73.6 5.0 copy-start.6
  73.9 6.1 copy-start.16
  73.9 207.1 %copy-start.17 = (s32[1,1,17]{2,1,0:T(1,128)S(1)}, s32[1,1,17]{2,1,0:T(1,128)}, u32[]{:S(2)}) copy-start(s32[1,1,17]{2,1,0:T(1,128)} %param.17) | copy-start | bytes 208
  78.6 206.8 %slice-start = ((bf16[408,16,512]{2,1,0:T(8,128)(2,1)}), bf16[24,16,512]{2,1,0:T(8,128)(2,1)S(1)}, s32[]{:S(2)}) async-start(bf16[408,16,512]{2,1,0:T(8,128)(2,1)} %gather_fusion.2), calls=%async_computation.7 | async-start | bytes 786432 | tf_op jit(solution)/shard_map/slice | solution.py:121
  280.0 11.6 %copy-start.8 = (pred[16,16]{1,0:T(8,128)(4,1)}, pred[16,16]{1,0:T(8,128)(4,1)S(1)}, u32[]{:S(2)}) copy-start(pred[16,16]{1,0:T(8,128)(4,1)S(1)} %get-tuple-element.7) | copy-start | bytes 772
  281.6 10.0 %copy-start.14 = (f32[64]{0:T(128)}, f32[64]{0:T(128)S(1)}, u32[]{:S(2)}) copy-start(f32[64]{0:T(128)S(1)} %multiply_power_fusion) | copy-start | bytes 772
  295.9 8.2 %copy-start.10 = (pred[16,2]{1,0:T(8,128)(4,1)S(1)}, pred[16,2]{1,0:T(8,128)(4,1)}, u32[]{:S(2)}) copy-start(pred[16,2]{1,0:T(8,128)(4,1)} %copy.101) | copy-start | bytes 100
  295.9 8.3 %copy-start.18 = (s32[1,1,17]{2,1,0:T(1,128)S(1)}, s32[1,1,17]{2,1,0:T(1,128)}, u32[]{:S(2)}) copy-start(s32[1,1,17]{2,1,0:T(1,128)} %param.17) | copy-start | bytes 208
  295.9 26.8 %copy-start.9 = (pred[16,16]{1,0:T(8,128)(4,1)S(1)}, pred[16,16]{1,0:T(8,128)(4,1)}, u32[]{:S(2)}) copy-start(pred[16,16]{1,0:T(8,128)(4,1)} %copy-done.8) | copy-start | bytes 772
  295.9 28.0 %copy-start.13 = (bf16[1536]{0:T(1024)(128)(2,1)S(1)}, bf16[1536]{0:T(1024)(128)(2,1)}, u32[]{:S(2)}) copy-start(bf16[1536]{0:T(1024)(128)(2,1)} %param.23) | copy-start | bytes 9220
  295.9 28.6 %copy-start.15 = (f32[64]{0:T(128)S(1)}, f32[64]{0:T(128)}, u32[]{:S(2)}) copy-start(f32[64]{0:T(128)} %copy-done.14) | copy-start | bytes 772
  328.9 4.0 copy-start.5
  329.0 4.0 copy-start.7
  373.4 127.1 %all-gather.8.cloned.1.call-start = ((), (), s32[]{:S(2)}) async-start(), calls=%async_computation.5 | async-start | bytes 3760128 | tf_op jit(solution)/shard_map/all_gather | solution.py:191
  374.1 249.1 %reduce-scatter.2.cloned.1.call-start = ((), (), s32[]{:S(2)}) async-start(), calls=%async_computation.6 | async-start | bytes 7520256 | tf_op jit(solution)/shard_map/reduce_scatter | solution.py:200
  521.4 104.7 %copy-start.1 = (bf16[1,1,16,1536]{3,2,1,0:T(8,128)(2,1)S(1)}, bf16[1,1,16,1536]{3,2,1,0:T(8,128)(2,1)}, u32[]{:S(2)}) copy-start(bf16[1,1,16,1536]{3,2,1,0:T(8,128)(2,1)} %param.14) | copy-start | bytes 147460
Sparse Core Ops, SparseCore 0:
  75.1 178.6 all-gather.5
  373.5 90.6 all-gather.3
  465.9 34.5 all-gather.7
  521.5 101.5 reduce-scatter.1
where the time goes:
time: 643 us; the launch traced here: 633 us
  blocking collectives  218 us (34%)
  waiting for transfers between devices  198 us (31%)
  local copies, waits for them, and re-layouts  80.6 us (13%)
  matrix products  66.2 us (10%)
  other arithmetic  42.4 us (7%)
  between operations  14.8 us (2%)
  starting transfers between devices  12.7 us (2%)
    all_gather x1, blocking collectives, shards(): lax.all_gather(destination, 'req', axis=1, tiled=True)  200 us
    reduce_scatter x1, waiting for transfers between devices, shards(): lax.psum_scatter(jnp.dot(hidden, full_down, preferred_element_type=jnp.fl...  94.1 us
    all_gather x1, waiting for transfers between devices, shards(): lax.all_gather(mlp_in, 'blk', axis=0, tiled=True)  89.8 us
    dot_general x1, matrix products, shards(): jnp.einsum('nd,dkf->nkf', lax.all_gather(mlp_in, 'blk', axis=0, tiled=Tru...  23.1 us
    gather x1, local copies, waits for them, and re-layouts, shards(): gathered = pool_rows[table_rows].reshape(slot_total + 1, -1, width_per_row)  22.5 us
    dot_general x1, matrix products, shards(): jnp.dot(hidden, full_down, preferred_element_type=jnp.float32)  20.9 us
    all_gather x1, blocking collectives, shards(): lax.all_gather(lengths, 'req', axis=1, tiled=True)  18.5 us
    select_n x2, other arithmetic, extend(): jnp.where(token_positions < limit, cache_rows, jnp.where(token_positions...  13.7 us
  transfers between devices with their start and end apart: 6, of which 3 were waited for; matrix products, arithmetic and copies ran while one was open for 26% of the time, Pallas kernels for 0%

commit v1 on v0

--- a/solution.py
+++ b/solution.py
@@ -115,18 +115,44 @@
     pool_rows = cache_pool[0, 0]
     table_rows = page_table[0, 0]
     width_per_row = pool_rows.shape[-1]
-    gathered = pool_rows[table_rows].reshape(slot_total + 1, -1, width_per_row)
-    cache_length = gathered.shape[1]
-    decode_caches = gathered[:slot_total]
-    context = gathered[slot_total]
+    cache_length = table_rows.shape[1] * pool_rows.shape[1]
+    context = pool_rows[table_rows[slot_total]].reshape(cache_length, width_per_row)
     context_length = lengths[0, 0, slot_total]
     slot_ids = jnp.arange(slot_total, dtype=jnp.int32)
-    all_dest, all_len = (
-        lax.all_gather(destination, "req", axis=1, tiled=True),
-        lax.all_gather(lengths, "req", axis=1, tiled=True),
-    )
-    all_dest = all_dest[0]
-    all_len = all_len[0]
+
+    local_down = jnp.transpose(down_weight)[:, None, :]
+    all_weights = lax.all_gather(
+        jnp.concatenate([gate_up, local_down], axis=1), "req", axis=0, tiled=True
+    )
+
+    send_dest = destination[0, 0]
+    decode_x = decode_rows[0, 0]
+    own_len = lengths[0, 0, :slot_total]
+    same_dest = send_dest[None, :] == send_dest[:, None]
+    earlier = same_dest & (slot_ids[None, :] < slot_ids[:, None])
+    within = jnp.sum(earlier.astype(jnp.int32), axis=1)
+    target = send_dest * CAP + within
+    flat_slots = jnp.arange(n_req * CAP, dtype=jnp.int32)
+    matches = target[None, :] == flat_slots[:, None]
+    picked = jnp.sum(jnp.where(matches, slot_ids[None, :], 0), axis=1)
+    send_pages = table_rows[picked]
+    send_cache = pool_rows[send_pages].reshape(n_req, CAP, cache_length, width_per_row)
+    send_x = decode_x[picked].reshape(n_req, CAP, -1)
+    send_len = jnp.broadcast_to(own_len[picked].reshape(n_req, CAP, 1), (n_req, CAP, 128))
+    recv_cache = lax.all_to_all(send_cache, "req", split_axis=0, concat_axis=0, tiled=True)
+    recv_x = lax.all_to_all(send_x, "req", split_axis=0, concat_axis=0, tiled=True)
+    recv_len = lax.all_to_all(send_len, "req", split_axis=0, concat_axis=0, tiled=True)
+
+    shift = jnp.mod(send_dest - own_index, n_req)
+    source = jnp.mod(own_index - shift, n_req)
+    order_key = source * slot_total + slot_ids
+    rank = jnp.sum((order_key[None, :] < order_key[:, None]).astype(jnp.int32), axis=1)
+    chosen = rank[None, :] == slot_ids[:, None]
+    arrival_order = jnp.sum(jnp.where(chosen, (source * CAP + within)[None, :], 0), axis=1)
+    got_cache = recv_cache.reshape(n_req * CAP, cache_length, width_per_row)[arrival_order]
+    got_x = recv_x.reshape(n_req * CAP, -1)[arrival_order]
+    got_length = recv_len.reshape(n_req * CAP, 128)[arrival_order, 0]
+
     prefill_x = prefill_rows[0, 0]
     prefill_count = prefill_x.shape[0]
     block_ids = jnp.arange(prefill_count, dtype=jnp.int32)
@@ -143,72 +169,42 @@
         axis=1,
     )
     prefill_att = attend(prefill_q[None], key_block[None], allowed[None])[0]
-    send_dest = destination[0, 0]
-    decode_x = decode_rows[0, 0]
-    earlier = (send_dest[None, :] == send_dest[:, None]) & (slot_ids[None, :] < slot_ids[:, None])
-    within = jnp.sum(earlier.astype(jnp.int32), axis=1)
-    target = send_dest * CAP + within
-    flat_slots = jnp.arange(n_req * CAP, dtype=jnp.int32)
-    matches = target[None, :] == flat_slots[:, None]
-    picked = jnp.sum(jnp.where(matches, slot_ids[None, :], 0), axis=1)
-    filled = jnp.any(matches, axis=1)
-    send_cache = jnp.where(
-        filled[:, None, None], decode_caches[picked], jnp.zeros((), jnp.bfloat16)
-    ).reshape(n_req, CAP, cache_length, width_per_row)
-    send_x = jnp.where(filled[:, None], decode_x[picked], jnp.zeros((), jnp.bfloat16)).reshape(
-        n_req, CAP, -1
-    )
-    recv_cache, recv_x = (
-        lax.all_to_all(send_cache, "req", split_axis=0, concat_axis=0, tiled=True),
-        lax.all_to_all(send_x, "req", split_axis=0, concat_axis=0, tiled=True),
-    )
-    arriving = all_dest == own_index
-    arrival_rank = jnp.cumsum(arriving.astype(jnp.int32), axis=1) - 1
-    cap_ids = jnp.arange(CAP, dtype=jnp.int32)
-    placed = arriving[:, None, :] & (arrival_rank[:, None, :] == cap_ids[None, :, None])
-    slot_lengths = jnp.sum(jnp.where(placed, all_len[:, None, :slot_total], 0), axis=2).reshape(-1)
-    valid = jnp.any(placed, axis=2).reshape(-1)
-    position = jnp.cumsum(valid.astype(jnp.int32)) - 1
-    chosen = valid[None, :] & (position[None, :] == slot_ids[:, None])
-    arrival_order = jnp.sum(jnp.where(chosen, flat_slots[None, :], 0), axis=1)
-    got_cache = recv_cache.reshape(n_req * CAP, cache_length, width_per_row)[arrival_order]
-    got_x = recv_x.reshape(n_req * CAP, -1)[arrival_order]
-    got_length = slot_lengths[arrival_order]
+    prefill_res = prefill_x.astype(jnp.float32) + jnp.dot(
+        prefill_att, outproj_weight, preferred_element_type=jnp.float32
+    )
+    prefill_out = feed_forward(prefill_res, mlp_gain, all_weights)
+
     decode_q, decode_kv = project(
         rms_scale(got_x, attn_gain), inproj_weight, inproj_bias, got_length
     )
     cache_after = extend(got_cache, decode_kv, got_length)
     decode_allowed = (cache_ids[None, :] <= got_length[:, None])[:, None, :]
     decode_att = attend(decode_q[:, None, :], cache_after, decode_allowed)[:, 0]
-    inputs_all = jnp.concatenate([prefill_x, got_x], axis=0)
-    attended = jnp.concatenate([prefill_att, decode_att], axis=0)
-    residual = inputs_all.astype(jnp.float32) + jnp.dot(
-        attended, outproj_weight, preferred_element_type=jnp.float32
-    )
+    decode_res = got_x.astype(jnp.float32) + jnp.dot(
+        decode_att, outproj_weight, preferred_element_type=jnp.float32
+    )
+    decode_out = feed_forward(decode_res, mlp_gain, all_weights)
+    return (
+        prefill_out[None, None],
+        decode_out[None, None],
+        cache_after[None, None],
+    )
+
+
+def feed_forward(residual, mlp_gain, all_weights):
     mlp_in = rms_scale(residual, mlp_gain)
-    full_gate_up, full_down = (
-        lax.all_gather(gate_up, "req", axis=0, tiled=True),
-        lax.all_gather(down_weight, "req", axis=1, tiled=True),
-    )
     gate_and_up = jnp.einsum(
         "nd,dkf->nkf",
         lax.all_gather(mlp_in, "blk", axis=0, tiled=True),
-        full_gate_up,
+        all_weights[:, :2, :],
         preferred_element_type=jnp.float32,
     )
     hidden = (jax.nn.silu(gate_and_up[:, 0, :]) * gate_and_up[:, 1, :]).astype(jnp.bfloat16)
-    mlp_rows = lax.psum_scatter(
-        jnp.dot(hidden, full_down, preferred_element_type=jnp.float32).astype(jnp.bfloat16),
-        "blk",
-        scatter_dimension=0,
-        tiled=True,
-    ).astype(jnp.float32)
-    layer_rows = (residual + mlp_rows).astype(jnp.bfloat16)
-    return (
-        layer_rows[:prefill_count][None, None],
-        layer_rows[prefill_count:][None, None],
-        cache_after[None, None],
-    )
+    partial = jnp.einsum(
+        "nf,df->nd", hidden, all_weights[:, 2, :], preferred_element_type=jnp.float32
+    ).astype(jnp.bfloat16)
+    mlp_rows = lax.psum_scatter(partial, "blk", scatter_dimension=0, tiled=True)
+    return (residual + mlp_rows.astype(jnp.float32)).astype(jnp.bfloat16)
 
 
 def solution(mesh):

time: 643 us -> 538 us (0.84)
  blocking collectives: 218 us -> 35.6 us
  waiting for transfers between devices: 198 us -> 278 us
  starting transfers between devices: 12.7 us -> 19.5 us
    all_gather x2 -> x1, blocking collectives: 218 us -> 35.6 us  [feed_forward(): lax.all_gather(mlp_in, 'blk', axis=0, tiled=True)]
    all_to_all x1, waiting for transfers between devices: 0.01 us -> 153 us  [shards(): lax.all_to_all(send_cache, 'req', split_axis=0, concat_axis=0, tiled=True)]
    all_gather x3 -> x2, waiting for transfers between devices: 103 us -> 0.02 us  [the longest x1 0.02 us: feed_forward(): lax.all_gather(mlp_in, 'blk', axis=0, tiled=True)]
    reduce_scatter x1 -> x2, waiting for transfers between devices: 94.1 us -> 125 us  [feed_forward(): mlp_rows = lax.psum_scatter(partial, 'blk', scatter_dimension=0, tiled=True)]
    select_n x5 -> x3, other arithmetic: 12.2 us -> 0.62 us  [the longest x1 0.61 us: shards(): pool_rows[send_pages].reshape(n_req, CAP, cache_length, width_per_row)]
    gather x5 -> x6, local copies, waits for them, and re-layouts: 33.3 us -> 29.5 us  [the longest x1 22.6 us: shards(): pool_rows[send_pages].reshape(n_req, CAP, cache_length, width_per_row)]
    dot_general x3 -> x6, matrix products: 48.4 us -> 50.5 us  [the longest x2 26.7 us: feed_forward(): jnp.einsum('nd,dkf->nkf', lax.all_gather(mlp_in, 'blk', axis=0, tiled=Tru...]
  transfers between devices with their start and end apart: 6 -> 7, of which waited for: 3 -> 3; matrix products, arithmetic and copies ran while one was open for 26% -> 34% of each run, Pallas kernels for 0% -> 0%
where the time goes in v1:
time: 538 us; the launch traced here: 531 us
  waiting for transfers between devices  278 us (52%)
  local copies, waits for them, and re-layouts  74.5 us (14%)
  matrix products  68.8 us (13%)
  other arithmetic  40.5 us (8%)
  blocking collectives  35.6 us (7%)
  starting transfers between devices  19.5 us (4%)
  between operations  14.6 us (3%)
    all_to_all x1, waiting for transfers between devices, shards(): lax.all_to_all(send_cache, 'req', split_axis=0, concat_axis=0, tiled=True)  153 us
    reduce_scatter x2, waiting for transfers between devices, feed_forward(): mlp_rows = lax.psum_scatter(partial, 'blk', scatter_dimension=0, tiled=True)  125 us
    all_gather x1, blocking collectives, feed_forward(): lax.all_gather(mlp_in, 'blk', axis=0, tiled=True)  35.6 us
    dot_general x2, matrix products, feed_forward(): jnp.einsum('nd,dkf->nkf', lax.all_gather(mlp_in, 'blk', axis=0, tiled=Tru...  26.7 us
    gather x1, local copies, waits for them, and re-layouts, shards(): pool_rows[send_pages].reshape(n_req, CAP, cache_length, width_per_row)  22.6 us
    dot_general x2, matrix products, feed_forward(): jnp.einsum('nf,df->nd', hidden, all_weights[:, 2, :], preferred_element_t...  19.1 us
    select_n x2, other arithmetic, extend(): jnp.where(token_positions < limit, cache_rows, jnp.where(token_positions...  13.7 us
  transfers between devices with their start and end apart: 7, of which 3 were waited for; matrix products, arithmetic and copies ran while one was open for 34% of the time, Pallas kernels for 0%

profile of v1, /device:TPU:0, one launch (start us, length us, event | category | flops | bytes accessed | tf_op | source)
XLA Modules:
  0.0 531.4 jit_solution(4753264827990152510)
XLA Ops:
  7.2 1.1 copy.83
  8.3 1.9 pad_maximum_fusion
  10.2 0.9 convert_reduce_fusion.1
  11.1 1.2 iota_add_fusion
  12.3 1.2 multiply_add_fusion
  13.6 0.7 slice_bitcast_fusion.5
  14.3 0.7 gather_fusion.3
  15.1 0.7 broadcast_in_dim.103
  15.8 6.4 %all-to-all-start.1 = ((s32[16,2,128]{2,1,0:T(2,128)}), s32[16,2,128]{2,1,0:T(2,128)S(1)}, u32[]{:S(2)}, u32[]{:S(2)}) async-start(s32[16,2,128]{2,1,0:T(2,128)} %broadcast_in_dim.103), calls=%async_computation.2 | async-start | bytes 32768 | tf_op jit(solution)/shard_map/all_to_all | solution.py:144
  22.2 0.7 convert_element_type.139
  22.9 0.7 convert_element_type.137
  23.6 1.4 fusion.14
  25.0 5.0 convolution_add_fusion.1
  30.0 0.7 slice.194
  31.3 1.3 slice.135
  32.8 0.6 add_convert_fusion.3
  33.7 0.8 copy.73
  34.6 3.1 copy.77
  37.7 3.6 gather_fusion
  42.2 1.4 maximum_multiply_fusion.1
  43.8 0.9 maximum_bitcast_fusion
  44.7 0.8 fusion.59
  45.5 1.0 slice_negate_fusion
  47.1 0.9 copy.74
  48.0 1.2 copy.75
  49.2 0.8 reshape.514
  50.0 1.4 gather_fusion.1
  51.4 1.6 reshape.454
  53.0 6.2 %all-to-all-start = ((bf16[16,2,1536]{2,1,0:T(2,128)(2,1)}), bf16[16,2,1536]{2,1,0:T(2,128)(2,1)}, u32[]{:S(2)}, u32[]{:S(2)}) async-start(bf16[16,2,1536]{2,1,0:T(2,128)(2,1)} %reshape.454), calls=%async_computation.1 | async-start | bytes 196608 | tf_op jit(solution)/shard_map/all_to_all | solution.py:143
  59.2 22.6 %gather_fusion.6 = bf16[768,16,512]{2,1,0:T(8,128)(2,1)} fusion(bf16[408,16,512]{2,1,0:T(8,128)(2,1)} %bitcast.183, s32[1024]{0:T(1024)S(1)} %pad_clamp_fusion), kind=kCustom, calls=%fused_computation.6 | custom fusion | bytes 25168896 | tf_op jit(solution)/shard_map/gather | solution.py:139
  81.8 5.9 %all-to-all-start.2 = ((bf16[16,2,384,512]{3,2,1,0:T(8,128)(2,1)}), bf16[16,2,384,512]{3,2,1,0:T(8,128)(2,1)}, u32[]{:S(2)}, u32[]{:S(2)}) async-start(bf16[16,2,384,512]{3,2,1,0:T(8,128)(2,1)} %bitcast.179), calls=%async_computation.3 | async-start | bytes 25165824 | tf_op jit(solution)/shard_map/all_to_all | solution.py:142
  88.2 2.4 maximum_multiply_fusion
  90.6 3.1 copy.78
  93.7 1.3 mul.270
  95.0 3.0 copy.76
  98.0 2.2 add_convert_fusion.1
  100.5 0.6 iota_compare_fusion.7
  101.3 1.3 fusion.7
  102.7 1.6 fusion.1
  104.4 2.5 fusion.17
  107.0 1.5 multiply_reduce_fusion
  108.5 1.1 multiply_convert_fusion
  110.1 0.7 gather_fusion.4
  111.2 0.9 reshape.455
  112.8 3.8 convolution_add_fusion.3
  117.3 152.8 %all-to-all-done.2 = bf16[16,2,384,512]{3,2,1,0:T(8,128)(2,1)} async-done(((bf16[16,2,384,512]{3,2,1,0:T(8,128)(2,1)}), bf16[16,2,384,512]{3,2,1,0:T(8,128)(2,1)}, u32[]{:S(2)}, u32[]{:S(2)}) %all-to-all-start.2) | async-done | bytes 12582944 | tf_op jit(solution)/shard_map/all_to_all | solution.py:142
  270.1 8.2 %gather_fusion.7 = bf16[16,384,512]{2,1,0:T(8,128)(2,1)} fusion(bf16[32,384,512]{2,1,0:T(8,128)(2,1)} %bitcast.41, s32[1024]{0:T(1024)S(1)} %pad_clamp_fusion.2), kind=kCustom, calls=%fused_computation.7 | custom fusion | bytes 12582976 | tf_op jit(solution)/shard_map/gather | solution.py:152
  278.3 6.1 %select_select_fusion = bf16[16,384,512]{2,1,0:T(8,128)(2,1)S(1)} fusion(bf16[16,384,512]{2,1,0:T(8,128)(2,1)} %gather_fusion.7, pred[16,384]{1,0:T(8,128)(4,1)S(1)} %get-tuple-element.25, pred[16,384]{1,0:T(8,128)(4,1)S(1)} %get-tuple-element.26, bf16[16,512]{1,0:T(8,128)(2,1)S(1)} %pad_maximum_fusion.3), kind=kLoop, calls=%fused_computation.18 | loop fusion | flops 6291456 | bytes 12611584 | tf_op jit(solution)/shard_map/jit(_where)/select_n | solution.py:90
  284.4 3.5 fusion.58
  287.9 4.7 copy.85
  292.6 4.7 copy.86
  297.3 2.6 fusion.60
  300.2 3.1 fusion.23
  303.4 3.2 multiply_reduce_fusion.1
  306.7 35.6 %all_gather.11 = bf16[128,1536]{1,0:T(8,128)(2,1)S(1)} all-gather(bf16[16,1536]{1,0:T(8,128)(2,1)S(1)} %multiply_convert_fusion.1), channel_id=1, replica_groups=mesh['req'=16,'blk'=8] {'blk'}, dimensions={0}, use_global_device_ids=true | all-gather | bytes 442368 | tf_op jit(solution)/shard_map/all_gather | solution.py:198
  342.3 5.9 %fusion.5 = f32[128,2,1120]{0,2,1:T(8,128)S(1)} fusion(bf16[1536,3,1120]{2,0,1:T(8,128)(2,1)} %all-gather.5.cloned.1.call-done, bf16[128,1536]{1,0:T(8,128)(2,1)S(1)} %all_gather.11), kind=kOutput, calls=%fused_computation.20 | convolution fusion | flops 880803840 | bytes 8617984 | tf_op jit(solution)/shard_map/nd,dkf->nkf/dot_general | solution.py:196
  348.2 4.1 fusion.13
  352.7 20.8 %fusion.2 = f32[2048,2,1120]{0,2,1:T(8,128)} fusion(bf16[2048,1536]{1,0:T(8,128)(2,1)} %all-gather.3.cloned.1.call-done, bf16[1536,3,1120]{2,0,1:T(8,128)(2,1)} %all-gather.5.cloned.1.call-done), kind=kOutput, calls=%fused_computation.16 | convolution fusion | flops 14092861440 | bytes 31719424 | tf_op jit(solution)/shard_map/nd,dkf->nkf/dot_general | solution.py:196
  373.4 15.0 %convolution_convert_fusion = bf16[2048,1536]{1,0:T(8,128)(2,1)} fusion(f32[2048,2,1120]{0,2,1:T(8,128)} %fusion.2, bf16[1536,3,1120]{2,0,1:T(8,128)(2,1)} %all-gather.5.cloned.1.call-done), kind=kOutput, calls=%fused_computation.13 | convolution fusion | flops 7063339008 | bytes 28180480 | tf_op jit(solution)/shard_map/nf,df->nd/dot_general | solution.py:203
  388.5 7.6 %bitcast_select_fusion.1 = bf16[1,1,16,384,512]{4,3,2,1,0:T(8,128)(2,1)} fusion(bf16[16,384,512]{2,1,0:T(8,128)(2,1)} %gather_fusion.7, pred[16,384]{1,0:T(8,128)(4,1)S(1)} %get-tuple-element.25, pred[16,384]{1,0:T(8,128)(4,1)S(1)} %get-tuple-element.26, bf16[16,512]{1,0:T(8,128)(2,1)S(1)} %pad_maximum_fusion.3), kind=kLoop, calls=%fused_computation.15 | loop fusion | flops 6291456 | bytes 12611584 | tf_op jit(solution)/shard_map/jit(_where)/select_n | solution.py:90
  396.1 25.4 %reduce-scatter.5.cloned.1.call-done = bf16[16,1536]{1,0:T(8,128)(2,1)} async-done(((bf16[128,1536]{1,0:T(8,128)(2,1)}), bf16[16,1536]{1,0:T(8,128)(2,1)}) %reduce-scatter.5.cloned.1.call-update) | async-done | bytes 49168 | tf_op jit(solution)/shard_map/reduce_scatter | solution.py:206
  421.5 1.4 fusion.41
  422.9 99.5 %reduce-scatter.3.cloned.1.call-done = bf16[256,1536]{1,0:T(8,128)(2,1)} async-done(((bf16[2048,1536]{1,0:T(8,128)(2,1)}), bf16[256,1536]{1,0:T(8,128)(2,1)}) %reduce-scatter.3.cloned.1.call-update) | async-done | bytes 786448 | tf_op jit(solution)/shard_map/reduce_scatter | solution.py:206
  522.4 2.2 fusion.24
  (109 shorter events, 7.2 us)
Async XLA Ops:
  7.2 42.9 %copy-start = (bf16[1,1,16,1536]{3,2,1,0:T(8,128)(2,1)S(1)}, bf16[1,1,16,1536]{3,2,1,0:T(8,128)(2,1)}, u32[]{:S(2)}) copy-start(bf16[1,1,16,1536]{3,2,1,0:T(8,128)(2,1)} %param.14) | copy-start | bytes 147460
  7.2 335.1 %all-gather.5.cloned.1.call-start = ((), (), s32[]{:S(2)}) async-start(), calls=%async_computation.6 | async-start | bytes 11280384 | tf_op jit(solution)/shard_map/all_gather | solution.py:124
  13.6 0.7 copy-start.10
  15.8 37.3 %all-to-all-start.1 = ((s32[16,2,128]{2,1,0:T(2,128)}), s32[16,2,128]{2,1,0:T(2,128)S(1)}, u32[]{:S(2)}, u32[]{:S(2)}) async-start(s32[16,2,128]{2,1,0:T(2,128)} %broadcast_in_dim.103), calls=%async_computation.2 | async-start | bytes 32768 | tf_op jit(solution)/shard_map/all_to_all | solution.py:144
  22.9 7.1 %copy-start.5 = (f32[2048]{0:T(1024)}, f32[2048]{0:T(1024)S(1)}, u32[]{:S(2)}) copy-start(f32[2048]{0:T(1024)S(1)} %convert_element_type.139) | copy-start | bytes 24580
  23.6 6.4 %copy-start.7 = (f32[1536]{0:T(1024)}, f32[1536]{0:T(1024)S(1)}, u32[]{:S(2)}) copy-start(f32[1536]{0:T(1024)S(1)} %convert_element_type.137) | copy-start | bytes 18436
  25.0 5.8 %copy-start.16 = (s32[1,1,17]{2,1,0:T(1,128)S(1)}, s32[1,1,17]{2,1,0:T(1,128)}, u32[]{:S(2)}) copy-start(s32[1,1,17]{2,1,0:T(1,128)} %param.17) | copy-start | bytes 208
  30.0 7.6 %copy-start.9 = (s32[1,1,17,24]{3,1,2,0:T(1,128)S(1)}, s32[1,1,17,24]{3,1,2,0:T(1,128)}, u32[]{:S(2)}) copy-start(s32[1,1,17,24]{3,1,2,0:T(1,128)} %param.16) | copy-start | bytes 4900
  32.8 4.9 copy-start.12
  41.9 3.6 copy-start.2
  53.0 28.8 %all-to-all-start = ((bf16[16,2,1536]{2,1,0:T(2,128)(2,1)}), bf16[16,2,1536]{2,1,0:T(2,128)(2,1)}, u32[]{:S(2)}, u32[]{:S(2)}) async-start(bf16[16,2,1536]{2,1,0:T(2,128)(2,1)} %reshape.454), calls=%async_computation.1 | async-start | bytes 196608 | tf_op jit(solution)/shard_map/all_to_all | solution.py:143
  81.8 188.3 %all-to-all-start.2 = ((bf16[16,2,384,512]{3,2,1,0:T(8,128)(2,1)}), bf16[16,2,384,512]{3,2,1,0:T(8,128)(2,1)}, u32[]{:S(2)}, u32[]{:S(2)}) async-start(bf16[16,2,384,512]{3,2,1,0:T(8,128)(2,1)} %bitcast.179), calls=%async_computation.3 | async-start | bytes 25165824 | tf_op jit(solution)/shard_map/all_to_all | solution.py:142
  87.7 265.0 %all-gather.3.cloned.1.call-start = ((), (), s32[]{:S(2)}) async-start(), calls=%async_computation.5 | async-start | bytes 7077888 | tf_op jit(solution)/shard_map/all_gather | solution.py:198
  93.7 6.8 %copy-start.11 = (bf16[1536]{0:T(1024)(128)(2,1)S(1)}, bf16[1536]{0:T(1024)(128)(2,1)}, u32[]{:S(2)}) copy-start(bf16[1536]{0:T(1024)(128)(2,1)} %param.23) | copy-start | bytes 9220
  102.6 1.7 copy-start.4
  102.7 4.2 slice-start
  104.3 2.6 slice-start.1
  104.3 2.6 copy-start.3
  106.9 2.9 copy-start.15
  106.9 3.1 copy-start.14
  106.9 3.9 copy-start.13
  106.9 5.9 %copy-start.6 = (f32[2048]{0:T(1024)S(1)}, f32[2048]{0:T(1024)}, u32[]{:S(2)}) copy-start(f32[2048]{0:T(1024)} %copy-done.5) | copy-start | bytes 24580
  106.9 5.9 %copy-start.8 = (f32[1536]{0:T(1024)S(1)}, f32[1536]{0:T(1024)}, u32[]{:S(2)}) copy-start(f32[1536]{0:T(1024)} %copy-done.7) | copy-start | bytes 18436
  109.6 311.9 %reduce-scatter.5.cloned.1.call-start = ((), (), s32[]{:S(2)}) async-start(), calls=%async_computation.8 | async-start | bytes 442368 | tf_op jit(solution)/shard_map/reduce_scatter | solution.py:206
  352.4 170.0 %reduce-scatter.3.cloned.1.call-start = ((), (), s32[]{:S(2)}) async-start(), calls=%async_computation.7 | async-start | bytes 7077888 | tf_op jit(solution)/shard_map/reduce_scatter | solution.py:206
  388.5 136.1 %copy-start.1 = (bf16[1,1,16,1536]{3,2,1,0:T(8,128)(2,1)S(1)}, bf16[1,1,16,1536]{3,2,1,0:T(8,128)(2,1)}, u32[]{:S(2)}) copy-start(bf16[1,1,16,1536]{3,2,1,0:T(8,128)(2,1)} %param.14) | copy-start | bytes 147460
Sparse Core Ops, SparseCore 0:
  10.3 66.3 all-gather.4
  109.7 132.6 all-gather.2
  352.5 68.9 reduce-scatter.4
  425.2 97.1 reduce-scatter.2

commit v2 on v1

--- a/solution.py
+++ b/solution.py
@@ -149,9 +149,6 @@
     rank = jnp.sum((order_key[None, :] < order_key[:, None]).astype(jnp.int32), axis=1)
     chosen = rank[None, :] == slot_ids[:, None]
     arrival_order = jnp.sum(jnp.where(chosen, (source * CAP + within)[None, :], 0), axis=1)
-    got_cache = recv_cache.reshape(n_req * CAP, cache_length, width_per_row)[arrival_order]
-    got_x = recv_x.reshape(n_req * CAP, -1)[arrival_order]
-    got_length = recv_len.reshape(n_req * CAP, 128)[arrival_order, 0]
 
     prefill_x = prefill_rows[0, 0]
     prefill_count = prefill_x.shape[0]
@@ -172,7 +169,14 @@
     prefill_res = prefill_x.astype(jnp.float32) + jnp.dot(
         prefill_att, outproj_weight, preferred_element_type=jnp.float32
     )
-    prefill_out = feed_forward(prefill_res, mlp_gain, all_weights)
+    prefill_partial = feed_forward_partial(prefill_res, mlp_gain, all_weights)
+    prefill_out = feed_forward_finish(prefill_res, prefill_partial)
+    prefill_out, recv_cache, recv_x, recv_len = lax.optimization_barrier(
+        (prefill_out, recv_cache, recv_x, recv_len)
+    )
+    got_cache = recv_cache.reshape(n_req * CAP, cache_length, width_per_row)[arrival_order]
+    got_x = recv_x.reshape(n_req * CAP, -1)[arrival_order]
+    got_length = recv_len.reshape(n_req * CAP, 128)[arrival_order, 0]
 
     decode_q, decode_kv = project(
         rms_scale(got_x, attn_gain), inproj_weight, inproj_bias, got_length
@@ -183,7 +187,9 @@
     decode_res = got_x.astype(jnp.float32) + jnp.dot(
         decode_att, outproj_weight, preferred_element_type=jnp.float32
     )
-    decode_out = feed_forward(decode_res, mlp_gain, all_weights)
+    decode_out = feed_forward_finish(
+        decode_res, feed_forward_partial(decode_res, mlp_gain, all_weights)
+    )
     return (
         prefill_out[None, None],
         decode_out[None, None],
@@ -191,7 +197,7 @@
     )
 
 
-def feed_forward(residual, mlp_gain, all_weights):
+def feed_forward_partial(residual, mlp_gain, all_weights):
     mlp_in = rms_scale(residual, mlp_gain)
     gate_and_up = jnp.einsum(
         "nd,dkf->nkf",
@@ -200,9 +206,12 @@
         preferred_element_type=jnp.float32,
     )
     hidden = (jax.nn.silu(gate_and_up[:, 0, :]) * gate_and_up[:, 1, :]).astype(jnp.bfloat16)
-    partial = jnp.einsum(
+    return jnp.einsum(
         "nf,df->nd", hidden, all_weights[:, 2, :], preferred_element_type=jnp.float32
     ).astype(jnp.bfloat16)
+
+
+def feed_forward_finish(residual, partial):
     mlp_rows = lax.psum_scatter(partial, "blk", scatter_dimension=0, tiled=True)
     return (residual + mlp_rows.astype(jnp.float32)).astype(jnp.bfloat16)
 

time: 538 us -> 620 us (1.15)
  waiting for transfers between devices: 278 us -> 377 us
  local copies, waits for them, and re-layouts: 74.5 us -> 67.6 us
  other arithmetic: 40.5 us -> 33.8 us
    all_gather x1, waiting for transfers between devices: 0.02 us -> 89.8 us  [feed_forward_partial(): lax.all_gather(mlp_in, 'blk', axis=0, tiled=True)]
    all_to_all x1, waiting for transfers between devices: 153 us -> 77 us  [shards(): lax.all_to_all(send_cache, 'req', split_axis=0, concat_axis=0, tiled=True)]
    all_gather x1, waiting for transfers between devices: 0.01 us -> 62.8 us  [shards(): lax.all_gather(jnp.concatenate([gate_up, local_down], axis=1), 'req', axi...]
    reduce_scatter x2, waiting for transfers between devices: 125 us -> 144 us  [feed_forward_finish(): mlp_rows = lax.psum_scatter(partial, 'blk', scatter_dimension=0, tiled=True)]
  transfers between devices with their start and end apart: 7 -> 7, of which waited for: 3 -> 6; matrix products, arithmetic and copies ran while one was open for 34% -> 6% of each run, Pallas kernels for 0% -> 0%
where the time goes in v2:
time: 620 us; the launch traced here: 611 us
  waiting for transfers between devices  377 us (61%)
  local copies, waits for them, and re-layouts  67.6 us (11%)
  matrix products  66.7 us (11%)
  blocking collectives  35.4 us (6%)
  other arithmetic  33.8 us (5%)
  starting transfers between devices  15.4 us (2%)
  between operations  14.6 us (2%)
    reduce_scatter x2, waiting for transfers between devices, feed_forward_finish(): mlp_rows = lax.psum_scatter(partial, 'blk', scatter_dimension=0, tiled=True)  144 us
    all_gather x1, waiting for transfers between devices, feed_forward_partial(): lax.all_gather(mlp_in, 'blk', axis=0, tiled=True)  89.8 us
    all_to_all x1, waiting for transfers between devices, shards(): lax.all_to_all(send_cache, 'req', split_axis=0, concat_axis=0, tiled=True)  77 us
    all_gather x1, waiting for transfers between devices, shards(): lax.all_gather(jnp.concatenate([gate_up, local_down], axis=1), 'req', axi...  62.8 us
    all_gather x1, blocking collectives, feed_forward_partial(): lax.all_gather(mlp_in, 'blk', axis=0, tiled=True)  35.4 us
    dot_general x2, matrix products, feed_forward_partial(): jnp.einsum('nd,dkf->nkf', lax.all_gather(mlp_in, 'blk', axis=0, tiled=Tru...  26.6 us
    gather x1, local copies, waits for them, and re-layouts, shards(): pool_rows[send_pages].reshape(n_req, CAP, cache_length, width_per_row)  22.3 us
    dot_general x2, matrix products, feed_forward_partial(): jnp.einsum('nf,df->nd', hidden, all_weights[:, 2, :], preferred_element_t...  19.1 us
  transfers between devices with their start and end apart: 7, of which 6 were waited for; matrix products, arithmetic and copies ran while one was open for 6% of the time, Pallas kernels for 0%

profile of v2, /device:TPU:0, one launch (start us, length us, event | category | flops | bytes accessed | tf_op | source)
XLA Modules:
  0.0 610.9 jit_solution(5679577874657452129)
XLA Ops:
  7.2 0.7 convert_element_type.137
  7.9 0.7 convert_element_type.139
  8.6 1.4 fusion.14
  10.0 4.9 convolution_add_fusion.1
  15.0 1.3 slice.135
  16.3 0.6 slice.88
  16.9 0.6 add_convert_fusion.3
  17.5 1.2 iota_compare_fusion.7
  19.4 0.3 slice_negate_fusion.1
  19.7 0.8 copy.72
  20.5 0.4 maximum_multiply_fusion.1
  20.8 1.0 mul.264
  21.9 3.5 gather_fusion
  25.5 0.8 fusion.58
  26.4 3.0 copy.77
  29.5 1.5 slice_negate_fusion
  30.9 1.3 maximum_multiply_fusion
  32.2 3.0 copy.78
  35.2 1.3 mul.270
  36.5 3.0 copy.76
  39.5 2.2 add_convert_fusion.1
  42.0 1.2 copy.74
  43.4 1.3 fusion.7
  44.7 1.6 fusion.1
  46.4 2.5 fusion.17
  49.0 1.5 multiply_reduce_fusion
  50.5 1.1 multiply_convert_fusion
  51.7 0.9 pad_maximum_fusion
  52.7 0.5 reduce-scatter.3.cloned.1.call-start
  53.2 89.8 %all-gather.3.cloned.1.call-done = bf16[2048,1536]{1,0:T(8,128)(2,1)} async-done(((bf16[256,1536]{1,0:T(8,128)(2,1)}), bf16[2048,1536]{1,0:T(8,128)(2,1)}) %all-gather.3.cloned.1.call-update) | async-done | bytes 6291472 | tf_op jit(solution)/shard_map/all_gather | solution.py:204
  143.0 62.8 %all-gather.5.cloned.1.call-done = bf16[1536,3,1120]{2,0,1:T(8,128)(2,1)} async-done(((bf16[96,3,1120]{2,0,1:T(8,128)(2,1)}), bf16[1536,3,1120]{2,0,1:T(8,128)(2,1)}) %all-gather.5.cloned.1.call-update) | async-done | bytes 10321936 | tf_op jit(solution)/shard_map/all_gather | solution.py:124
  205.8 20.7 %fusion.2 = f32[2048,2,1120]{0,2,1:T(8,128)} fusion(bf16[2048,1536]{1,0:T(8,128)(2,1)} %all-gather.3.cloned.1.call-done, bf16[1536,3,1120]{2,0,1:T(8,128)(2,1)} %all-gather.5.cloned.1.call-done), kind=kOutput, calls=%fused_computation.16 | convolution fusion | flops 14092861440 | bytes 31719424 | tf_op jit(solution)/shard_map/nd,dkf->nkf/dot_general | solution.py:202
  226.5 15.0 %convolution_convert_fusion = bf16[2048,1536]{1,0:T(8,128)(2,1)} fusion(f32[2048,2,1120]{0,2,1:T(8,128)} %fusion.2, bf16[1536,3,1120]{2,0,1:T(8,128)(2,1)} %all-gather.5.cloned.1.call-done), kind=kOutput, calls=%fused_computation.13 | convolution fusion | flops 7063339008 | bytes 28180480 | tf_op jit(solution)/shard_map/nf,df->nd/dot_general | solution.py:209
  241.9 0.3 copy-done.11
  242.2 0.7 gather_fusion.4
  243.0 0.7 broadcast_in_dim.97
  243.7 5.0 all-to-all-start.2
  248.8 0.6 gather_fusion.1
  249.5 0.6 gather_fusion.3
  250.1 0.7 reshape.455
  250.8 4.1 all-to-all-done.2
  254.9 3.7 all-to-all-start.1
  258.6 22.3 %gather_fusion.2 = bf16[768,16,512]{2,1,0:T(8,128)(2,1)} fusion(bf16[408,16,512]{2,1,0:T(8,128)(2,1)} %bitcast.182, s32[1024]{0:T(1024)S(1)} %pad_clamp_fusion.2), kind=kCustom, calls=%fused_computation.2 | custom fusion | bytes 25168896 | tf_op jit(solution)/shard_map/gather | solution.py:139
  280.9 5.8 all-to-all-start
  287.3 82.0 %reduce-scatter.3.cloned.1.call-done = bf16[256,1536]{1,0:T(8,128)(2,1)} async-done(((bf16[2048,1536]{1,0:T(8,128)(2,1)}), bf16[256,1536]{1,0:T(8,128)(2,1)}) %reduce-scatter.3.cloned.1.call-update) | async-done | bytes 786448 | tf_op jit(solution)/shard_map/reduce_scatter | solution.py:215
  369.4 2.2 add_convert_fusion
  371.6 77.0 %all-to-all-done = bf16[16,2,384,512]{3,2,1,0:T(8,128)(2,1)} async-done(((bf16[16,2,384,512]{3,2,1,0:T(8,128)(2,1)}), bf16[16,2,384,512]{3,2,1,0:T(8,128)(2,1)}, u32[]{:S(2)}, u32[]{:S(2)}) %all-to-all-start) | async-done | bytes 12582944 | tf_op jit(solution)/shard_map/all_to_all | solution.py:142
  448.6 0.6 gather_fusion.5
  449.3 3.8 convolution_add_fusion.3
  453.1 0.7 gather_fusion.6
  454.3 8.2 %gather_fusion.7 = bf16[16,384,512]{2,1,0:T(8,128)(2,1)} fusion(bf16[32,384,512]{2,1,0:T(8,128)(2,1)} %bitcast.41, s32[1024]{0:T(1024)S(1)} %pad_clamp_fusion), kind=kCustom, calls=%fused_computation.7 | custom fusion | bytes 12582976 | tf_op jit(solution)/shard_map/gather | solution.py:177
  463.1 6.1 %select_select_fusion = bf16[16,384,512]{2,1,0:T(8,128)(2,1)S(1)} fusion(bf16[16,384,512]{2,1,0:T(8,128)(2,1)} %gather_fusion.7, pred[16,384]{1,0:T(8,128)(4,1)S(1)} %get-tuple-element.33, pred[16,384]{1,0:T(8,128)(4,1)S(1)} %get-tuple-element.34, bf16[16,512]{1,0:T(8,128)(2,1)S(1)} %pad_maximum_fusion.3), kind=kLoop, calls=%fused_computation.18 | loop fusion | flops 6291456 | bytes 12611584 | tf_op jit(solution)/shard_map/jit(_where)/select_n | solution.py:90
  469.2 3.4 fusion.57
  472.6 3.4 copy.86
  476.0 4.7 copy.85
  480.6 0.8 fusion.59
  481.6 3.1 fusion.23
  484.9 3.2 multiply_reduce_fusion.1
  488.1 35.4 %all_gather.11 = bf16[128,1536]{1,0:T(8,128)(2,1)S(1)} all-gather(bf16[16,1536]{1,0:T(8,128)(2,1)S(1)} %multiply_convert_fusion.1), channel_id=1, replica_groups=mesh['req'=16,'blk'=8] {'blk'}, dimensions={0}, use_global_device_ids=true | all-gather | bytes 442368 | tf_op jit(solution)/shard_map/all_gather | solution.py:204
  523.5 5.8 fusion.5
  529.4 4.1 fusion.13
  533.5 7.6 %bitcast_select_fusion.1 = bf16[1,1,16,384,512]{4,3,2,1,0:T(8,128)(2,1)} fusion(bf16[16,384,512]{2,1,0:T(8,128)(2,1)} %gather_fusion.7, pred[16,384]{1,0:T(8,128)(4,1)S(1)} %get-tuple-element.33, pred[16,384]{1,0:T(8,128)(4,1)S(1)} %get-tuple-element.34, bf16[16,512]{1,0:T(8,128)(2,1)S(1)} %pad_maximum_fusion.3), kind=kLoop, calls=%fused_computation.15 | loop fusion | flops 6291456 | bytes 12611584 | tf_op jit(solution)/shard_map/jit(_where)/select_n | solution.py:90
  541.1 61.6 %reduce-scatter.5.cloned.1.call-done = bf16[16,1536]{1,0:T(8,128)(2,1)} async-done(((bf16[128,1536]{1,0:T(8,128)(2,1)}), bf16[16,1536]{1,0:T(8,128)(2,1)}) %reduce-scatter.5.cloned.1.call-update) | async-done | bytes 49168 | tf_op jit(solution)/shard_map/reduce_scatter | solution.py:215
  602.7 1.4 fusion.40
  (99 shorter events, 4.3 us)
Async XLA Ops:
  7.2 242.3 %copy-start = (bf16[1,1,16,1536]{3,2,1,0:T(8,128)(2,1)S(1)}, bf16[1,1,16,1536]{3,2,1,0:T(8,128)(2,1)}, u32[]{:S(2)}) copy-start(bf16[1,1,16,1536]{3,2,1,0:T(8,128)(2,1)} %param.14) | copy-start | bytes 147460
  7.2 135.8 %all-gather.3.cloned.1.call-start = ((), (), s32[]{:S(2)}) async-start(), calls=%async_computation.5 | async-start | bytes 7077888 | tf_op jit(solution)/shard_map/all_gather | solution.py:204
  7.2 11.5 %copy-start.6 = (f32[64]{0:T(128)}, f32[64]{0:T(128)S(1)}, u32[]{:S(2)}) copy-start(f32[64]{0:T(128)S(1)} %multiply_power_fusion) | copy-start | bytes 772
  10.0 6.3 %copy-start.10 = (s32[1,1,17]{2,1,0:T(1,128)S(1)}, s32[1,1,17]{2,1,0:T(1,128)}, u32[]{:S(2)}) copy-start(s32[1,1,17]{2,1,0:T(1,128)} %param.17) | copy-start | bytes 208
  14.9 5.5 copy-start.4
  35.2 8.0 %copy-start.9 = (pred[384]{0:T(512)(128)(4,1)S(1)}, pred[384]{0:T(512)(128)(4,1)}, u32[]{:S(2)}) copy-start(pred[384]{0:T(512)(128)(4,1)} %iota_compare_fusion.7) | copy-start | bytes 1156
  44.7 4.2 slice-start
  46.3 2.6 slice-start.1
  46.4 2.6 copy-start.1
  48.9 1.6 copy-start.5
  48.9 2.7 copy-start.2
  49.0 2.8 copy-start.3
  49.0 4.2 copy-start.8
  51.6 154.2 %all-gather.5.cloned.1.call-start = ((), (), s32[]{:S(2)}) async-start(), calls=%async_computation.6 | async-start | bytes 11280384 | tf_op jit(solution)/shard_map/all_gather | solution.py:124
  52.7 316.7 %reduce-scatter.3.cloned.1.call-start = ((), (), s32[]{:S(2)}) async-start(), calls=%async_computation.7 | async-start | bytes 7077888 | tf_op jit(solution)/shard_map/reduce_scatter | solution.py:215
  241.6 0.7 copy-start.11
  243.7 11.1 %all-to-all-start.2 = ((s32[16,2,128]{2,1,0:T(2,128)}), s32[16,2,128]{2,1,0:T(2,128)S(1)}, u32[]{:S(2)}, u32[]{:S(2)}) async-start(s32[16,2,128]{2,1,0:T(2,128)} %broadcast_in_dim.97), calls=%async_computation.3 | async-start | bytes 32768 | tf_op jit(solution)/shard_map/all_to_all | solution.py:144
  254.9 26.0 %all-to-all-start.1 = ((bf16[16,2,1536]{2,1,0:T(2,128)(2,1)}), bf16[16,2,1536]{2,1,0:T(2,128)(2,1)S(1)}, u32[]{:S(2)}, u32[]{:S(2)}) async-start(bf16[16,2,1536]{2,1,0:T(2,128)(2,1)} %reshape.455), calls=%async_computation.2 | async-start | bytes 196608 | tf_op jit(solution)/shard_map/all_to_all | solution.py:143
  280.9 167.7 %all-to-all-start = ((bf16[16,2,384,512]{3,2,1,0:T(8,128)(2,1)}), bf16[16,2,384,512]{3,2,1,0:T(8,128)(2,1)}, u32[]{:S(2)}, u32[]{:S(2)}) async-start(bf16[16,2,384,512]{3,2,1,0:T(8,128)(2,1)} %bitcast.178), calls=%async_computation.1 | async-start | bytes 25165824 | tf_op jit(solution)/shard_map/all_to_all | solution.py:142
  286.7 167.3 %copy-start.7 = (f32[64]{0:T(128)S(1)}, f32[64]{0:T(128)}, u32[]{:S(2)}) copy-start(f32[64]{0:T(128)} %copy-done.6) | copy-start | bytes 772
  286.7 316.0 %reduce-scatter.5.cloned.1.call-start = ((), (), s32[]{:S(2)}) async-start(), calls=%async_computation.8 | async-start | bytes 442368 | tf_op jit(solution)/shard_map/reduce_scatter | solution.py:215
Sparse Core Ops, SparseCore 0:
  51.7 91.2 all-gather.2
  145.2 60.5 all-gather.4
  241.7 127.5 reduce-scatter.2
  533.6 69.0 reduce-scatter.4
